TPU v7x, 256 devices: a whole 4x4x8 slice. The times are simulated.
256 devices in a mesh: seq: 16 (over z, y_hi), roll: 16 (over y_lo, x, core).
Axes of the slice: x: 4, y: 4 (y_hi: 2, y_lo: 2; y = y_hi * 2 + y_lo), z: 8, core: 2. Of those that a mesh axis runs over, the one named last changes fastest.
Arguments:
- tokens: int32 [16, 7936], P('roll', 'seq'), may hold values from 0 to 29
- breaks: int32 [16, 7936], P('roll', 'seq'), may hold values 0 or 1
- lengths: int32 [16], P('roll'), may hold values from 3968 to 7936, as said below
- embed_table: float32 [30, 1280], replicated, may hold values from -6 to 6
- break_vec: float32 [1280], replicated, may hold values from -6 to 6
- gain_in: float32 [2, 1280], replicated, may hold values from 0.25 to 1.75
- gain_mid: float32 [2, 640], replicated, may hold values from 0.25 to 1.75
- gain_out: float32 [2, 640], replicated, may hold values from 0.25 to 1.75
- w_in: bfloat16 [2, 1280, 640], P(None, 'roll'), may hold values from -0.15625 to 0.15625
- convolution_weight: bfloat16 [2, 640, 3200], P(None, 'roll'), may hold values from -0.109375 to 0.109375
- w_out: bfloat16 [2, 640, 1280], P(None, 'roll'), may hold values from -0.25 to 0.25
Outputs:
- encoded: bfloat16 [16, 7936, 1280], P('roll', 'seq')
Inputs may be any that keep to these rules, and one draw needn't show every extreme that they name: `lengths`: some complex has all 7936 residues valid in every draw.
All inputs are finite; a program needn't handle non-finite values. No bound on the sum of `breaks` on one device may be relied on, other than what follows from the above.
Results may differ from a plain program's by a relative error of at most 0.014.
Values may be sent and summed in bfloat16 or wider, within the bound.
A program may use at most 64 MiB of HBM per device.

v0:
```python
import functools

import jax
import numpy as np
import jax.numpy as jnp
from jax import lax
from jax.experimental import pallas as pl
from jax.experimental.pallas import tpu as pltpu
from jax.sharding import Mesh, PartitionSpec as P

H = 640
KERNEL = 5
VOCAB = 30
BLOCKS = 2
BASE_DILATION = 64
ROLL = ("ylo", "x", "core")
MESH = pl.DeviceIdType.MESH


def halo_kernel(reach, x_ref, zeros_ref, out_ref, send_sem, recv_sem, local_sem):
    n_seq = lax.axis_size("seq")
    seq_i = lax.axis_index("seq")
    ylo = lax.axis_index("ylo")
    x = lax.axis_index("x")
    c = lax.axis_index("core")
    rows = x_ref.shape[0]
    has_prev = seq_i > 0
    has_next = seq_i < n_seq - 1
    prev = (seq_i - 1, ylo, x, c)
    nxt = (seq_i + 1, ylo, x, c)

    barrier = pltpu.get_barrier_semaphore()

    n_peers = (seq_i + n_seq - 1) // n_seq + (2 * n_seq - 2 - seq_i) // n_seq

    @pl.when(has_prev)
    def _():
        pl.semaphore_signal(barrier, inc=1, device_id=prev, device_id_type=MESH)

    @pl.when(has_next)
    def _():
        pl.semaphore_signal(barrier, inc=1, device_id=nxt, device_id_type=MESH)

    pl.semaphore_wait(barrier, n_peers)

    to_next = pltpu.make_async_remote_copy(
        src_ref=x_ref.at[pl.ds(rows - reach, reach)],
        dst_ref=out_ref.at[pl.ds(0, reach)],
        send_sem=send_sem.at[0],
        recv_sem=recv_sem.at[0],
        device_id=nxt,
        device_id_type=MESH,
    )
    to_prev = pltpu.make_async_remote_copy(
        src_ref=x_ref.at[pl.ds(0, reach)],
        dst_ref=out_ref.at[pl.ds(rows + reach, reach)],
        send_sem=send_sem.at[1],
        recv_sem=recv_sem.at[1],
        device_id=prev,
        device_id_type=MESH,
    )
    from_prev = pltpu.make_async_remote_copy(
        src_ref=x_ref.at[pl.ds(rows - reach, reach)],
        dst_ref=out_ref.at[pl.ds(0, reach)],
        send_sem=send_sem.at[0],
        recv_sem=recv_sem.at[0],
        device_id=prev,
        device_id_type=MESH,
    )
    from_next = pltpu.make_async_remote_copy(
        src_ref=x_ref.at[pl.ds(0, reach)],
        dst_ref=out_ref.at[pl.ds(rows + reach, reach)],
        send_sem=send_sem.at[1],
        recv_sem=recv_sem.at[1],
        device_id=nxt,
        device_id_type=MESH,
    )
    middle = pltpu.make_async_copy(x_ref, out_ref.at[pl.ds(reach, rows)], local_sem.at[0])
    head = pltpu.make_async_copy(zeros_ref, out_ref.at[pl.ds(0, reach)], local_sem.at[1])
    tail = pltpu.make_async_copy(zeros_ref, out_ref.at[pl.ds(rows + reach, reach)], local_sem.at[2])

    @pl.when(has_next)
    def _():
        to_next.start()

    @pl.when(has_prev)
    def _():
        to_prev.start()

    middle.start()

    @pl.when(jnp.logical_not(has_prev))
    def _():
        head.start()

    @pl.when(jnp.logical_not(has_next))
    def _():
        tail.start()

    middle.wait()

    @pl.when(has_next)
    def _():
        to_next.wait_send()
        from_next.wait_recv()

    @pl.when(has_prev)
    def _():
        to_prev.wait_send()
        from_prev.wait_recv()

    @pl.when(jnp.logical_not(has_prev))
    def _():
        head.wait()

    @pl.when(jnp.logical_not(has_next))
    def _():
        tail.wait()


def extend_halo(x, reach, collective_id):
    rows, width = x.shape
    zeros = jnp.zeros((reach, width), x.dtype)
    any_spec = pl.BlockSpec(memory_space=pl.ANY)
    return pl.pallas_call(
        functools.partial(halo_kernel, reach),
        out_shape=jax.ShapeDtypeStruct((rows + 2 * reach, width), x.dtype),
        in_specs=[any_spec, any_spec],
        out_specs=any_spec,
        scratch_shapes=[
            pltpu.SemaphoreType.DMA((2,)),
            pltpu.SemaphoreType.DMA((2,)),
            pltpu.SemaphoreType.DMA((3,)),
        ],
        compiler_params=pltpu.CompilerParams(
            collective_id=collective_id, has_side_effects=True
        ),
    )(x, zeros)


def layer_norm(values, gain):
    center = jnp.mean(values, axis=-1, keepdims=True)
    spread = jnp.mean((values - center) ** 2, axis=-1, keepdims=True)
    return (values - center) * lax.rsqrt(spread + 1e-05) * gain


def norm_gelu_rows(hidden_ref, gain_ref, normed_ref):
    rows = 16
    gain = gain_ref[...]

    def body(i, carry):
        span = pl.ds(pl.multiple_of(i * rows, rows), rows)
        values = hidden_ref[span, :].astype(jnp.float32)
        t = layer_norm(values, gain)
        gelu = 0.5 * t * (1.0 + lax.erf(t * np.float32(np.sqrt(0.5))))
        normed_ref[span, :] = gelu.astype(normed_ref.dtype)
        return carry

    lax.fori_loop(0, hidden_ref.shape[0] // rows, body, 0)


def gather_kernel(w_in_ref, conv_ref, w_out_ref, hidden_ref, gain_ref, in_out, conv_out, w_out_out, normed_ref, send_sem, recv_sem, local_sem):
    n_x = lax.axis_size("x")
    k_in = w_in_ref.shape[1]
    k_mid = conv_ref.shape[1]
    seq_i = lax.axis_index("seq")
    ylo = lax.axis_index("ylo")
    x = lax.axis_index("x")
    c = lax.axis_index("core")
    z = seq_i // 2
    y = (seq_i % 2) * 2 + ylo
    other = 1 - ylo

    def slot(par, xx, cc):
        return (par * n_x + xx) * 2 + cc

    def y_dev(yy):
        return (z * 2 + yy // 2, yy % 2, x, c)

    x_right = lax.rem(x + 1, n_x)
    x_left = lax.rem(x + n_x - 1, n_x)
    x_far = lax.rem(x + 2, n_x)
    right = (seq_i, ylo, x_right, c)
    left = (seq_i, ylo, x_left, c)
    up = y_dev(lax.rem(y + 1, 4))
    down = y_dev(lax.rem(y + 3, 4))
    partner = (seq_i, ylo, x, 1 - c)

    barrier = pltpu.get_barrier_semaphore()
    for dev in (right, left, up, down, partner):
        pl.semaphore_signal(barrier, inc=1, device_id=dev, device_id_type=MESH)
    pl.semaphore_wait(barrier, 5)

    def pieces(s, b):
        rows_in = pl.ds(pl.multiple_of(s * k_in, 8), k_in)
        rows_mid = pl.ds(pl.multiple_of(s * k_mid, 8), k_mid)
        dst = [in_out.at[b, rows_in]]
        dst += [conv_out.at[b, k, rows_mid] for k in range(KERNEL)]
        dst += [w_out_out.at[b, rows_mid]]
        return dst

    def own_pieces(b):
        src = [w_in_ref.at[b]]
        src += [conv_ref.at[b, :, pl.ds(k * H, H)] for k in range(KERNEL)]
        src += [w_out_ref.at[b]]
        return src

    sends = []

    def send(s, b, dev, own=False):
        dst = pieces(s, b)
        src = own_pieces(b) if own else dst
        for i, (a, d) in enumerate(zip(src, dst)):
            cp = pltpu.make_async_remote_copy(
                src_ref=a,
                dst_ref=d,
                send_sem=send_sem.at[len(sends)],
                recv_sem=recv_sem.at[s, b, i],
                device_id=dev,
                device_id_type=MESH,
            )
            cp.start()
            sends.append(cp)

    def arrive(s, b, dev):
        for i, d in enumerate(pieces(s, b)):
            pltpu.make_async_remote_copy(
                src_ref=d,
                dst_ref=d,
                send_sem=send_sem.at[0],
                recv_sem=recv_sem.at[s, b, i],
                device_id=dev,
                device_id_type=MESH,
            ).wait_recv()

    me = slot(ylo, x, c)
    for h in range(2):
        send(me, h, right, own=True)
    for h in range(2):
        send(me, h, left, own=True)
    send(me, 0, up, own=True)
    send(me, 1, down, own=True)
    for h in range(2):
        send(me, h, partner, own=True)
    locals_ = []
    for h in range(2):
        for a, d in zip(own_pieces(h), pieces(me, h)):
            cp = pltpu.make_async_copy(a, d, local_sem.at[len(locals_)])
            cp.start()
            locals_.append(cp)

    norm_gelu_rows(hidden_ref, gain_ref, normed_ref)

    s_left = slot(ylo, x_left, c)
    s_right = slot(ylo, x_right, c)
    for h in range(2):
        arrive(s_left, h, left)
    send(s_left, 0, right)
    send(s_left, 0, up)
    send(s_left, 1, down)
    for h in range(2):
        arrive(s_right, h, right)
    send(s_right, 1, left)
    send(s_right, 0, up)
    send(s_right, 1, down)
    for s in (s_left, s_right):
        for h in range(2):
            send(s, h, partner)

    s_far = slot(ylo, x_far, c)
    arrive(s_far, 0, left)
    arrive(s_far, 1, right)
    send(s_far, 0, up)
    send(s_far, 1, down)
    for h in range(2):
        send(s_far, h, partner)

    for xx in (x, x_left, x_right, x_far):
        s = slot(other, xx, c)
        arrive(s, 0, down)
        arrive(s, 1, up)
        for h in range(2):
            send(s, h, partner)

    for par in (ylo, other):
        for xx in (x, x_left, x_right, x_far):
            s = slot(par, xx, 1 - c)
            for h in range(2):
                arrive(s, h, partner)
    for cp in sends:
        cp.wait_send()
    for cp in locals_:
        cp.wait()


def gather_weights(w_in, conv, w_out, hidden, gain, n_slots):
    blocks, k_in, _ = w_in.shape
    k_mid = conv.shape[1]
    d_model = w_out.shape[2]
    n_pieces = KERNEL + 2
    any_spec = pl.BlockSpec(memory_space=pl.ANY)
    vmem_spec = pl.BlockSpec(memory_space=pltpu.VMEM)
    return pl.pallas_call(
        gather_kernel,
        out_shape=(
            jax.ShapeDtypeStruct((blocks, n_slots * k_in, H), w_in.dtype),
            jax.ShapeDtypeStruct((blocks, KERNEL, n_slots * k_mid, H), conv.dtype),
            jax.ShapeDtypeStruct((blocks, n_slots * k_mid, d_model), w_out.dtype),
            jax.ShapeDtypeStruct(hidden.shape, jnp.bfloat16),
        ),
        in_specs=[any_spec] * 3 + [vmem_spec] * 2,
        out_specs=(any_spec,) * 3 + (vmem_spec,),
        scratch_shapes=[
            pltpu.SemaphoreType.DMA((30 * n_pieces,)),
            pltpu.SemaphoreType.DMA((n_slots, blocks, n_pieces)),
            pltpu.SemaphoreType.DMA((blocks * n_pieces,)),
        ],
        compiler_params=pltpu.CompilerParams(collective_id=0, has_side_effects=True),
    )(w_in, conv, w_out, hidden, gain)


def per_device(
    tokens,
    breaks,
    lengths,
    embed_table,
    break_vec,
    gain_in,
    gain_mid,
    gain_out,
    w_in,
    convolution_weight,
    w_out,
):
    local_rows = tokens.shape[1]
    complexes = tokens.shape[0]
    seq_place = lax.axis_index("seq")
    k_in = w_in.shape[1]
    k_mid = convolution_weight.shape[1]
    d_model = w_out.shape[2]
    halves = d_model // H
    n_slots = lax.axis_size("ylo") * lax.axis_size("x") * lax.axis_size("core")


    onehot = (tokens[:, :, None] == jnp.arange(VOCAB, dtype=jnp.int32)[None, None, :]).astype(
        jnp.float32
    )
    hidden_state = jnp.einsum(
        "cnv,vd->cnd",
        onehot,
        embed_table,
        precision=lax.Precision.HIGHEST,
        preferred_element_type=jnp.float32,
    )
    hidden_state = (
        hidden_state + breaks[:, :, None].astype(jnp.float32) * break_vec[None, None, :]
    ).astype(jnp.bfloat16)
    in_all, conv_all, out_all, normed_first = gather_weights(
        w_in, convolution_weight, w_out, hidden_state[0], gain_in[0:1], n_slots
    )
    position = seq_place * local_rows + jnp.arange(local_rows, dtype=jnp.int32)
    valid_rows = ((position[None, :] >= 0) & (position[None, :] < lengths[:, None])).astype(
        jnp.float32
    )
    for block_number in range(BLOCKS):
        dilation_step = BASE_DILATION * 2**block_number
        reach_rows = KERNEL // 2 * dilation_step
        in_full = in_all[block_number]
        if block_number == 0:
            normed = normed_first.reshape(hidden_state.shape)
        else:
            normed = jax.nn.gelu(
                layer_norm(hidden_state.astype(jnp.float32), gain_in[block_number]),
                approximate=False,
            ).astype(jnp.bfloat16)
            normed = lax.optimization_barrier(normed)
        padded_hidden = jnp.einsum(
            "cnd,dh->cnh", normed, in_full, preferred_element_type=jnp.float32
        )
        conv_input = (
            jax.nn.gelu(layer_norm(padded_hidden, gain_mid[block_number]), approximate=False)
            * valid_rows[:, :, None]
        ).astype(jnp.bfloat16)
        extended = extend_halo(conv_input[0], reach_rows, 1 + block_number)[None]
        mixed = jnp.zeros((complexes, local_rows, H), jnp.float32)
        for tap in range(KERNEL):
            tap_w = conv_all[block_number, tap]
            window = extended[:, tap * dilation_step : tap * dilation_step + local_rows]
            mixed = mixed + jnp.einsum(
                "cnh,hg->cng", window, tap_w, preferred_element_type=jnp.float32
            )
        activated = jax.nn.gelu(
            layer_norm(mixed, gain_out[block_number]), approximate=False
        ).astype(jnp.bfloat16)
        activated = lax.optimization_barrier(activated)
        out_full = out_all[block_number]
        update = jnp.einsum(
            "cnh,hd->cnd", activated, out_full, preferred_element_type=jnp.float32
        )
        hidden_state = (hidden_state.astype(jnp.float32) + update).astype(jnp.bfloat16)
    return hidden_state


def solution(mesh):
    seq_size, roll_size = mesh.devices.shape
    devices = mesh.devices.reshape(seq_size, roll_size // 8, 4, 2)
    fine = Mesh(devices, ("seq",) + ROLL)
    placed = (
        P(ROLL, "seq"),
        P(ROLL, "seq"),
        P(ROLL),
        P(),
        P(),
        P(),
        P(),
        P(),
        P(None, ROLL, None),
        P(None, ROLL, None),
        P(None, ROLL, None),
    )
    return jax.shard_map(
        per_device, mesh=fine, in_specs=placed, out_specs=P(ROLL, "seq", None), check_vma=False
    )
```

profile of v0, /device:TPU:1, one launch (start us, length us, event | category | flops | bytes accessed | tf_op | source)
XLA Modules:
  0.0 183.6 jit_solution(13613588444031994808)
XLA Ops:
  0.0 0.7 convert_element_type.70
  0.9 3.0 %fusion.2.hidden_ref = bf16[496,1280]{1,0:T(8,128)(2,1)} fusion(f32[30,1280]{1,0:T(8,128)S(1)} %copy-done, f32[1280]{0:T(1024)} %param.15, f32[496]{0:T(512)S(1)} %bitcast.125, s32[496]{0:T(512)} %bitcast.126), kind=kOutput, calls=%fused_computation.8 | convolution fusion | flops 230476320 | bytes 1432448 | tf_op jit(solution)/shard_map/cnv,vd->cnd/dot_general | solution.py:348
  3.9 0.6 slice_reduce_fusion
  4.5 67.7 %shard_map.109 = (bf16[2,1280,640]{2,1,0:T(8,128)(2,1)}, bf16[2,5,640,640]{3,2,1,0:T(8,128)(2,1)}, bf16[2,640,1280]{2,1,0:T(8,128)(2,1)}, bf16[496,1280]{1,0:T(8,128)(2,1)}) custom-call(bf16[2,80,640]{2,1,0:T(8,128)(2,1)} %w_in_ref.1, bf16[2,40,3200]{2,1,0:T(8,128)(2,1)} %conv_ref.1, bf16[2,40,1280]{2,1,0:T(8,128)(2,1)} %w_out_ref.1, ...), custom_call_target="tpu_custom_call" | custom-call | tf_op jit(solution)/shard_map/pallas_call | solution.py:303
  72.2 3.1 %fusion.109 = (f32[496]{0:T(512)S(1)}, f32[496,640]{1,0:T(8,128)S(1)}) fusion(bf16[496,1280]{1,0:T(8,128)(2,1)} %get-tuple-element.9, bf16[2,1280,640]{2,1,0:T(8,128)(2,1)} %get-tuple-element.10), kind=kOutput, calls=%fused_computation.200 | convolution fusion | flops 812963328 | bytes 4179904 | tf_op jit(solution)/shard_map/cnd,dh->cnh/dot_general | solution.py:377
  75.6 0.4 copy-done.5
  76.7 4.1 %fusion.37.x_ref = bf16[496,640]{1,0:T(8,128)(2,1)} fusion(f32[496,640]{1,0:T(8,128)S(1)} %get-tuple-element.20, f32[496]{0:T(512)S(1)} %fusion.108, f32[640]{0:T(1024)S(1)} %get-tuple-element.14, f32[496]{0:T(512)S(1)} %add_rsqrt_fusion.4, f32[496]{0:T(512)S(1)} %broadcast_multiply_fusion.4), kind=kLoop, calls=%fused_computation.61 | loop fusion | flops 21903360 | bytes 1913152 | tf_op jit(solution)/shard_map/convert_element_type | solution.py:383
  80.8 0.7 broadcast_in_dim.8.zeros_ref
  81.5 26.5 %shard_map.110 = bf16[752,640]{1,0:T(8,128)(2,1)} custom-call(bf16[496,640]{1,0:T(8,128)(2,1)} %fusion.37.x_ref, bf16[128,640]{1,0:T(8,128)(2,1)} %broadcast_in_dim.8.zeros_ref), custom_call_target="tpu_custom_call" | custom-call | tf_op jit(solution)/shard_map/pallas_call | solution.py:125
  108.0 2.2 %fusion.88 = f32[496,640]{1,0:T(8,128)S(1)} fusion(bf16[2,5,640,640]{3,2,1,0:T(8,128)(2,1)} %get-tuple-element.11, bf16[1,752,640]{2,1,0:T(8,128)(2,1)} %bitcast.115), kind=kOutput, calls=%fused_computation.152 | convolution fusion | flops 406323200 | bytes 2723840 | tf_op jit(solution)/shard_map/cnh,hg->cng/dot_general | solution.py:389
  110.2 1.9 %convolution_add_fusion.9 = f32[496,640]{1,0:T(8,128)S(1)} fusion(f32[496,640]{1,0:T(8,128)S(1)} %fusion.88, bf16[2,5,640,640]{3,2,1,0:T(8,128)(2,1)} %get-tuple-element.11, bf16[1,752,640]{2,1,0:T(8,128)(2,1)S(1)} %bitcast.116), kind=kOutput, calls=%fused_computation.57 | convolution fusion | flops 406640640 | bytes 3993600 | tf_op jit(solution)/shard_map/cnh,hg->cng/dot_general | solution.py:389
  112.1 1.9 %convolution_add_fusion.8 = f32[496,640]{1,0:T(8,128)S(1)} fusion(f32[496,640]{1,0:T(8,128)S(1)} %convolution_add_fusion.9, bf16[2,5,640,640]{3,2,1,0:T(8,128)(2,1)} %get-tuple-element.11, bf16[1,752,640]{2,1,0:T(8,128)(2,1)S(1)} %bitcast.117), kind=kOutput, calls=%fused_computation.56 | convolution fusion | flops 406640640 | bytes 3993600 | tf_op jit(solution)/shard_map/cnh,hg->cng/dot_general | solution.py:389
  114.0 1.9 %convolution_add_fusion.7 = f32[496,640]{1,0:T(8,128)S(1)} fusion(f32[496,640]{1,0:T(8,128)S(1)} %convolution_add_fusion.8, bf16[2,5,640,640]{3,2,1,0:T(8,128)(2,1)} %get-tuple-element.11, bf16[1,752,640]{2,1,0:T(8,128)(2,1)S(1)} %bitcast.118), kind=kOutput, calls=%fused_computation.55 | convolution fusion | flops 406640640 | bytes 3993600 | tf_op jit(solution)/shard_map/cnh,hg->cng/dot_general | solution.py:389
  115.9 2.2 %fusion.110 = (f32[496]{0:T(512)S(1)}, f32[496,640]{1,0:T(8,128)S(1)}) fusion(f32[496,640]{1,0:T(8,128)S(1)} %convolution_add_fusion.7, bf16[2,5,640,640]{3,2,1,0:T(8,128)(2,1)} %get-tuple-element.11, bf16[1,752,640]{2,1,0:T(8,128)(2,1)S(1)} %bitcast.119), kind=kOutput, calls=%fused_computation.201 | convolution fusion | flops 406957568 | bytes 3995584 | tf_op jit(solution)/shard_map/cnh,hg->cng/dot_general | solution.py:389
  118.4 0.4 copy-done.6
  118.8 3.5 %fusion.103 = bf16[1,496,640]{2,1,0:T(8,128)(2,1)S(1)} fusion(f32[640]{0:T(1024)S(1)} %get-tuple-element.16, f32[496]{0:T(512)S(1)} %add_rsqrt_fusion.3, f32[496,640]{1,0:T(8,128)S(1)} %get-tuple-element.22, f32[496]{0:T(512)S(1)} %broadcast_multiply_fusion.3), kind=kLoop, calls=%fused_computation.177 | loop fusion | flops 21585920 | bytes 1911168 | tf_op jit(solution)/shard_map/convert_element_type | solution.py:394
  122.3 1.3 convert_reduce_fusion
  123.6 0.5 fusion.6
  124.1 6.6 %fusion.48 = bf16[1,496,1280]{2,1,0:T(8,128)(2,1)S(1)} fusion(bf16[496,1280]{1,0:T(8,128)(2,1)S(1)} %get-tuple-element.24, f32[1280]{0:T(1024)S(1)} %get-tuple-element.17, f32[496]{0:T(512)S(1)} %add_rsqrt_fusion.2, f32[496]{0:T(512)S(1)} %broadcast_multiply_fusion), kind=kLoop, calls=%fused_computation.72 | loop fusion | flops 43806720 | bytes 2548608 | tf_op jit(solution)/shard_map/convert_element_type | solution.py:375
  130.7 1.3 fusion.111
  131.9 0.3 multiply_reduce_fusion.1
  132.2 4.1 %fusion.44.x_ref = bf16[496,640]{1,0:T(8,128)(2,1)} fusion(f32[496,640]{1,0:T(8,128)S(1)} %get-tuple-element.26, f32[640]{0:T(1024)S(1)} %get-tuple-element.13, f32[496]{0:T(512)S(1)} %add_rsqrt_fusion.1, f32[496]{0:T(512)S(1)} %broadcast_multiply_fusion.2, f32[496]{0:T(512)S(1)} %fusion.108), kind=kLoop, calls=%fused_computation.68 | loop fusion | flops 21903360 | bytes 1913152 | tf_op jit(solution)/shard_map/convert_element_type | solution.py:383
  136.4 0.8 broadcast_in_dim.10.zeros_ref
  137.1 30.3 %shard_map.111 = bf16[1008,640]{1,0:T(8,128)(2,1)} custom-call(bf16[496,640]{1,0:T(8,128)(2,1)} %fusion.44.x_ref, bf16[256,640]{1,0:T(8,128)(2,1)} %broadcast_in_dim.10.zeros_ref), custom_call_target="tpu_custom_call" | custom-call | tf_op jit(solution)/shard_map/pallas_call | solution.py:125
  167.5 2.2 %fusion.82 = f32[496,640]{1,0:T(8,128)S(1)} fusion(bf16[2,5,640,640]{3,2,1,0:T(8,128)(2,1)} %get-tuple-element.11, bf16[1,1008,640]{2,1,0:T(8,128)(2,1)} %bitcast.120), kind=kOutput, calls=%fused_computation.146 | convolution fusion | flops 406323200 | bytes 2723840 | tf_op jit(solution)/shard_map/cnh,hg->cng/dot_general | solution.py:389
  169.7 1.9 %convolution_add_fusion.5 = f32[496,640]{1,0:T(8,128)S(1)} fusion(f32[496,640]{1,0:T(8,128)S(1)} %fusion.82, bf16[2,5,640,640]{3,2,1,0:T(8,128)(2,1)} %get-tuple-element.11, bf16[1,1008,640]{2,1,0:T(8,128)(2,1)S(1)} %bitcast.121), kind=kOutput, calls=%fused_computation.53 | convolution fusion | flops 406640640 | bytes 3993600 | tf_op jit(solution)/shard_map/cnh,hg->cng/dot_general | solution.py:389
  171.6 1.9 %convolution_add_fusion.4 = f32[496,640]{1,0:T(8,128)S(1)} fusion(f32[496,640]{1,0:T(8,128)S(1)} %convolution_add_fusion.5, bf16[2,5,640,640]{3,2,1,0:T(8,128)(2,1)} %get-tuple-element.11, bf16[1,1008,640]{2,1,0:T(8,128)(2,1)S(1)} %bitcast.122), kind=kOutput, calls=%fused_computation.52 | convolution fusion | flops 406640640 | bytes 3993600 | tf_op jit(solution)/shard_map/cnh,hg->cng/dot_general | solution.py:389
  173.5 1.9 %convolution_add_fusion.3 = f32[496,640]{1,0:T(8,128)S(1)} fusion(f32[496,640]{1,0:T(8,128)S(1)} %convolution_add_fusion.4, bf16[2,5,640,640]{3,2,1,0:T(8,128)(2,1)} %get-tuple-element.11, bf16[1,1008,640]{2,1,0:T(8,128)(2,1)S(1)} %bitcast.123), kind=kOutput, calls=%fused_computation.51 | convolution fusion | flops 406640640 | bytes 3993600 | tf_op jit(solution)/shard_map/cnh,hg->cng/dot_general | solution.py:389
  175.5 2.2 %fusion.112 = (f32[496]{0:T(512)S(1)}, f32[496,640]{1,0:T(8,128)S(1)}) fusion(f32[496,640]{1,0:T(8,128)S(1)} %convolution_add_fusion.3, bf16[2,5,640,640]{3,2,1,0:T(8,128)(2,1)} %get-tuple-element.11, bf16[1,1008,640]{2,1,0:T(8,128)(2,1)S(1)} %bitcast.124), kind=kOutput, calls=%fused_computation.203 | convolution fusion | flops 406957568 | bytes 3995584 | tf_op jit(solution)/shard_map/cnh,hg->cng/dot_general | solution.py:389
  177.6 0.3 multiply_reduce_fusion
  177.9 3.5 %fusion.102 = bf16[1,496,640]{2,1,0:T(8,128)(2,1)S(1)} fusion(f32[640]{0:T(1024)S(1)} %get-tuple-element.15, f32[496]{0:T(512)S(1)} %add_rsqrt_fusion, f32[496,640]{1,0:T(8,128)S(1)} %get-tuple-element.28, f32[496]{0:T(512)S(1)} %broadcast_multiply_fusion.1), kind=kLoop, calls=%fused_computation.176 | loop fusion | flops 21585920 | bytes 1911168 | tf_op jit(solution)/shard_map/convert_element_type | solution.py:394
  181.4 2.2 %fusion.5 = bf16[1,496,1280]{2,1,0:T(8,128)(2,1)} fusion(bf16[496,1280]{1,0:T(8,128)(2,1)S(1)} %get-tuple-element.24, bf16[2,640,1280]{2,1,0:T(8,128)(2,1)S(1)} %copy-done.8, bf16[1,496,640]{2,1,0:T(8,128)(2,1)S(1)} %fusion.102), kind=kOutput, calls=%fused_computation.11 | convolution fusion | flops 814551040 | bytes 4812800 | tf_op jit(solution)/shard_map/cnh,hd->cnd/dot_general | solution.py:397
  (33 shorter events, 0.9 us)
Async XLA Ops:
  0.0 0.9 copy-start
  0.0 3.9 %copy-start.4 = (f32[2,1280]{1,0:T(2,128)S(1)}, f32[2,1280]{1,0:T(2,128)}, u32[]{:S(2)}) copy-start(f32[2,1280]{1,0:T(2,128)} %param.16) | copy-start | bytes 30724
  75.3 0.7 copy-start.5
  108.0 2.2 %copy-start.1 = (bf16[752,640]{1,0:T(8,128)(2,1)S(1)}, bf16[752,640]{1,0:T(8,128)(2,1)}, u32[]{:S(2)}) copy-start(bf16[752,640]{1,0:T(8,128)(2,1)} %shard_map.110) | copy-start | bytes 2887684
  115.9 6.4 %copy-start.7 = (bf16[2,640,1280]{2,1,0:T(8,128)(2,1)S(1)}, bf16[2,640,1280]{2,1,0:T(8,128)(2,1)}, u32[]{:S(2)}) copy-start(bf16[2,640,1280]{2,1,0:T(8,128)(2,1)} %get-tuple-element.12) | copy-start | bytes 9830404
  118.1 0.7 copy-start.6
  118.4 3.9 %copy-start.3 = (bf16[496,1280]{1,0:T(8,128)(2,1)S(1)}, bf16[496,1280]{1,0:T(8,128)(2,1)}, u32[]{:S(2)}) copy-start(bf16[496,1280]{1,0:T(8,128)(2,1)} %fusion.2.hidden_ref) | copy-start | bytes 3809284
  123.6 7.1 %copy-start.9 = (bf16[2,1280,640]{2,1,0:T(8,128)(2,1)S(1)}, bf16[2,1280,640]{2,1,0:T(8,128)(2,1)}, u32[]{:S(2)}) copy-start(bf16[2,1280,640]{2,1,0:T(8,128)(2,1)} %get-tuple-element.10) | copy-start | bytes 9830404
  167.5 2.2 %copy-start.2 = (bf16[1008,640]{1,0:T(8,128)(2,1)S(1)}, bf16[1008,640]{1,0:T(8,128)(2,1)}, u32[]{:S(2)}) copy-start(bf16[1008,640]{1,0:T(8,128)(2,1)} %shard_map.111) | copy-start | bytes 3870724
  175.4 6.0 %copy-start.8 = (bf16[2,640,1280]{2,1,0:T(8,128)(2,1)S(1)}, bf16[2,640,1280]{2,1,0:T(8,128)(2,1)}, u32[]{:S(2)}) copy-start(bf16[2,640,1280]{2,1,0:T(8,128)(2,1)} %get-tuple-element.12) | copy-start | bytes 9830404
where the time goes:
time: 184 us
  Pallas kernels  125 us (68%)
  matrix products  31 us (17%)
  other arithmetic  24.2 us (13%)
  local copies, waits for them, and re-layouts  3.09 us (2%)
    pallas_call x1, Pallas kernels, gather_weights(): pl.pallas_call(gather_kernel, out_shape=(jax.ShapeDtypeStruct((blocks, n_...  67.7 us
    pallas_call x2, Pallas kernels, extend_halo(): pl.pallas_call(functools.partial(halo_kernel, reach), out_shape=jax.Shape...  56.8 us
    dot_general x10, matrix products, per_device(): jnp.einsum('cnh,hg->cng', window, tap_w, preferred_element_type=jnp.float32)  20.2 us
    convert_element_type x2, other arithmetic, per_device(): conv_input = (jax.nn.gelu(layer_norm(padded_hidden, gain_mid[block_number...  8.27 us
    convert_element_type x2, other arithmetic, per_device(): activated = jax.nn.gelu(layer_norm(mixed, gain_out[block_number]), approx...  6.91 us
    convert_element_type x1, other arithmetic, per_device(): normed = jax.nn.gelu(layer_norm(hidden_state.astype(jnp.float32), gain_in...  6.57 us
    dot_general x2, matrix products, per_device(): jnp.einsum('cnd,dh->cnh', normed, in_full, preferred_element_type=jnp.flo...  4.31 us

commit v1 on v0

--- a/solution.py
+++ b/solution.py
@@ -17,7 +17,7 @@
 MESH = pl.DeviceIdType.MESH
 
 
-def halo_kernel(reach, x_ref, zeros_ref, out_ref, send_sem, recv_sem, local_sem):
+def halo_kernel(reach, x_ref, out_ref, send_sem, recv_sem):
     n_seq = lax.axis_size("seq")
     seq_i = lax.axis_index("seq")
     ylo = lax.axis_index("ylo")
@@ -30,7 +30,6 @@
     nxt = (seq_i + 1, ylo, x, c)
 
     barrier = pltpu.get_barrier_semaphore()
-
     n_peers = (seq_i + n_seq - 1) // n_seq + (2 * n_seq - 2 - seq_i) // n_seq
 
     @pl.when(has_prev)
@@ -43,9 +42,11 @@
 
     pl.semaphore_wait(barrier, n_peers)
 
+    head = out_ref.at[pl.ds(0, reach)]
+    tail = out_ref.at[pl.ds(rows + reach, reach)]
     to_next = pltpu.make_async_remote_copy(
         src_ref=x_ref.at[pl.ds(rows - reach, reach)],
-        dst_ref=out_ref.at[pl.ds(0, reach)],
+        dst_ref=head,
         send_sem=send_sem.at[0],
         recv_sem=recv_sem.at[0],
         device_id=nxt,
@@ -53,7 +54,7 @@
     )
     to_prev = pltpu.make_async_remote_copy(
         src_ref=x_ref.at[pl.ds(0, reach)],
-        dst_ref=out_ref.at[pl.ds(rows + reach, reach)],
+        dst_ref=tail,
         send_sem=send_sem.at[1],
         recv_sem=recv_sem.at[1],
         device_id=prev,
@@ -61,7 +62,7 @@
     )
     from_prev = pltpu.make_async_remote_copy(
         src_ref=x_ref.at[pl.ds(rows - reach, reach)],
-        dst_ref=out_ref.at[pl.ds(0, reach)],
+        dst_ref=head,
         send_sem=send_sem.at[0],
         recv_sem=recv_sem.at[0],
         device_id=prev,
@@ -69,15 +70,12 @@
     )
     from_next = pltpu.make_async_remote_copy(
         src_ref=x_ref.at[pl.ds(0, reach)],
-        dst_ref=out_ref.at[pl.ds(rows + reach, reach)],
+        dst_ref=tail,
         send_sem=send_sem.at[1],
         recv_sem=recv_sem.at[1],
         device_id=nxt,
         device_id_type=MESH,
     )
-    middle = pltpu.make_async_copy(x_ref, out_ref.at[pl.ds(reach, rows)], local_sem.at[0])
-    head = pltpu.make_async_copy(zeros_ref, out_ref.at[pl.ds(0, reach)], local_sem.at[1])
-    tail = pltpu.make_async_copy(zeros_ref, out_ref.at[pl.ds(rows + reach, reach)], local_sem.at[2])
 
     @pl.when(has_next)
     def _():
@@ -87,17 +85,15 @@
     def _():
         to_prev.start()
 
-    middle.start()
+    out_ref[pl.ds(reach, rows), :] = x_ref[...]
 
     @pl.when(jnp.logical_not(has_prev))
     def _():
-        head.start()
+        head[...] = jnp.zeros(head.shape, head.dtype)
 
     @pl.when(jnp.logical_not(has_next))
     def _():
-        tail.start()
-
-    middle.wait()
+        tail[...] = jnp.zeros(tail.shape, tail.dtype)
 
     @pl.when(has_next)
     def _():
@@ -109,33 +105,23 @@
         to_prev.wait_send()
         from_prev.wait_recv()
 
-    @pl.when(jnp.logical_not(has_prev))
-    def _():
-        head.wait()
-
-    @pl.when(jnp.logical_not(has_next))
-    def _():
-        tail.wait()
-
 
 def extend_halo(x, reach, collective_id):
     rows, width = x.shape
-    zeros = jnp.zeros((reach, width), x.dtype)
-    any_spec = pl.BlockSpec(memory_space=pl.ANY)
+    vmem_spec = pl.BlockSpec(memory_space=pltpu.VMEM)
     return pl.pallas_call(
         functools.partial(halo_kernel, reach),
         out_shape=jax.ShapeDtypeStruct((rows + 2 * reach, width), x.dtype),
-        in_specs=[any_spec, any_spec],
-        out_specs=any_spec,
+        in_specs=[vmem_spec],
+        out_specs=vmem_spec,
         scratch_shapes=[
             pltpu.SemaphoreType.DMA((2,)),
             pltpu.SemaphoreType.DMA((2,)),
-            pltpu.SemaphoreType.DMA((3,)),
         ],
         compiler_params=pltpu.CompilerParams(
             collective_id=collective_id, has_side_effects=True
         ),
-    )(x, zeros)
+    )(x)
 
 
 def layer_norm(values, gain):

time: 184 us -> 161 us (0.88)
  the two profiles are of different devices: /device:TPU:1 before, /device:TPU:216 now
where the time goes in v1:
time: 161 us; the launch traced here: 158 us
  Pallas kernels  100 us (62%)
  matrix products  31 us (19%)
  other arithmetic  24.2 us (15%)
  local copies, waits for them, and re-layouts  1.64 us (1%)
    pallas_call x1, Pallas kernels, gather_weights(): pl.pallas_call(gather_kernel, out_shape=(jax.ShapeDtypeStruct((blocks, n_...  65.1 us
    pallas_call x2, Pallas kernels, extend_halo(): pl.pallas_call(functools.partial(halo_kernel, reach), out_shape=jax.Shape...  34.9 us
    dot_general x10, matrix products, per_device(): jnp.einsum('cnh,hg->cng', window, tap_w, preferred_element_type=jnp.float32)  20.2 us
    convert_element_type x2, other arithmetic, per_device(): conv_input = (jax.nn.gelu(layer_norm(padded_hidden, gain_mid[block_number...  8.27 us
    convert_element_type x2, other arithmetic, per_device(): activated = jax.nn.gelu(layer_norm(mixed, gain_out[block_number]), approx...  6.91 us
    convert_element_type x1, other arithmetic, per_device(): normed = jax.nn.gelu(layer_norm(hidden_state.astype(jnp.float32), gain_in...  6.57 us
    dot_general x2, matrix products, per_device(): jnp.einsum('cnd,dh->cnh', normed, in_full, preferred_element_type=jnp.flo...  4.31 us
    dot_general x2, matrix products, per_device(): jnp.einsum('cnh,hd->cnd', activated, out_full, preferred_element_type=jnp...  3.48 us

profile of v1, /device:TPU:216, one launch (start us, length us, event | category | flops | bytes accessed | tf_op | source)
XLA Modules:
  0.0 157.7 jit_solution(6977095366990010634)
XLA Ops:
  0.0 0.7 convert_element_type.70
  0.9 3.0 %fusion.2.hidden_ref = bf16[496,1280]{1,0:T(8,128)(2,1)} fusion(f32[30,1280]{1,0:T(8,128)S(1)} %copy-done, f32[1280]{0:T(1024)} %param.15, f32[496]{0:T(512)S(1)} %bitcast.125, s32[496]{0:T(512)} %bitcast.126), kind=kOutput, calls=%fused_computation.8 | convolution fusion | flops 230476320 | bytes 1432448 | tf_op jit(solution)/shard_map/cnv,vd->cnd/dot_general | solution.py:334
  3.9 0.6 slice_reduce_fusion
  4.5 65.1 %shard_map.109 = (bf16[2,1280,640]{2,1,0:T(8,128)(2,1)}, bf16[2,5,640,640]{3,2,1,0:T(8,128)(2,1)}, bf16[2,640,1280]{2,1,0:T(8,128)(2,1)}, bf16[496,1280]{1,0:T(8,128)(2,1)}) custom-call(bf16[2,80,640]{2,1,0:T(8,128)(2,1)} %w_in_ref.1, bf16[2,40,3200]{2,1,0:T(8,128)(2,1)} %conv_ref.1, bf16[2,40,1280]{2,1,0:T(8,128)(2,1)} %w_out_ref.1, ...), custom_call_target="tpu_custom_call" | custom-call | tf_op jit(solution)/shard_map/pallas_call | solution.py:289
  69.6 3.1 %fusion.109 = (f32[496]{0:T(512)S(1)}, f32[496,640]{1,0:T(8,128)S(1)}) fusion(bf16[496,1280]{1,0:T(8,128)(2,1)} %get-tuple-element.9, bf16[2,1280,640]{2,1,0:T(8,128)(2,1)} %get-tuple-element.10), kind=kOutput, calls=%fused_computation.200 | convolution fusion | flops 812963328 | bytes 4179904 | tf_op jit(solution)/shard_map/cnd,dh->cnh/dot_general | solution.py:363
  72.7 0.3 multiply_reduce_fusion.3
  73.0 0.4 copy-done.5
  74.0 4.1 %fusion.37.x_ref = bf16[496,640]{1,0:T(8,128)(2,1)} fusion(f32[496,640]{1,0:T(8,128)S(1)} %get-tuple-element.20, f32[496]{0:T(512)S(1)} %fusion.108, f32[640]{0:T(1024)S(1)} %get-tuple-element.14, f32[496]{0:T(512)S(1)} %add_rsqrt_fusion.4, f32[496]{0:T(512)S(1)} %broadcast_multiply_fusion.4), kind=kLoop, calls=%fused_computation.61 | loop fusion | flops 21903360 | bytes 1913152 | tf_op jit(solution)/shard_map/convert_element_type | solution.py:369
  78.2 14.3 %shard_map.110 = bf16[752,640]{1,0:T(8,128)(2,1)} custom-call(bf16[496,640]{1,0:T(8,128)(2,1)} %fusion.37.x_ref), custom_call_target="tpu_custom_call" | custom-call | tf_op jit(solution)/shard_map/pallas_call | solution.py:112
  92.5 2.2 %fusion.88 = f32[496,640]{1,0:T(8,128)S(1)} fusion(bf16[2,5,640,640]{3,2,1,0:T(8,128)(2,1)} %get-tuple-element.11, bf16[1,752,640]{2,1,0:T(8,128)(2,1)} %bitcast.115), kind=kOutput, calls=%fused_computation.152 | convolution fusion | flops 406323200 | bytes 2723840 | tf_op jit(solution)/shard_map/cnh,hg->cng/dot_general | solution.py:375
  94.7 1.9 %convolution_add_fusion.9 = f32[496,640]{1,0:T(8,128)S(1)} fusion(f32[496,640]{1,0:T(8,128)S(1)} %fusion.88, bf16[2,5,640,640]{3,2,1,0:T(8,128)(2,1)} %get-tuple-element.11, bf16[1,752,640]{2,1,0:T(8,128)(2,1)S(1)} %bitcast.116), kind=kOutput, calls=%fused_computation.57 | convolution fusion | flops 406640640 | bytes 3993600 | tf_op jit(solution)/shard_map/cnh,hg->cng/dot_general | solution.py:375
  96.6 1.9 %convolution_add_fusion.8 = f32[496,640]{1,0:T(8,128)S(1)} fusion(f32[496,640]{1,0:T(8,128)S(1)} %convolution_add_fusion.9, bf16[2,5,640,640]{3,2,1,0:T(8,128)(2,1)} %get-tuple-element.11, bf16[1,752,640]{2,1,0:T(8,128)(2,1)S(1)} %bitcast.117), kind=kOutput, calls=%fused_computation.56 | convolution fusion | flops 406640640 | bytes 3993600 | tf_op jit(solution)/shard_map/cnh,hg->cng/dot_general | solution.py:375
  98.5 1.9 %convolution_add_fusion.7 = f32[496,640]{1,0:T(8,128)S(1)} fusion(f32[496,640]{1,0:T(8,128)S(1)} %convolution_add_fusion.8, bf16[2,5,640,640]{3,2,1,0:T(8,128)(2,1)} %get-tuple-element.11, bf16[1,752,640]{2,1,0:T(8,128)(2,1)S(1)} %bitcast.118), kind=kOutput, calls=%fused_computation.55 | convolution fusion | flops 406640640 | bytes 3993600 | tf_op jit(solution)/shard_map/cnh,hg->cng/dot_general | solution.py:375
  100.5 2.2 %fusion.110 = (f32[496]{0:T(512)S(1)}, f32[496,640]{1,0:T(8,128)S(1)}) fusion(f32[496,640]{1,0:T(8,128)S(1)} %convolution_add_fusion.7, bf16[2,5,640,640]{3,2,1,0:T(8,128)(2,1)} %get-tuple-element.11, bf16[1,752,640]{2,1,0:T(8,128)(2,1)S(1)} %bitcast.119), kind=kOutput, calls=%fused_computation.201 | convolution fusion | flops 406957568 | bytes 3995584 | tf_op jit(solution)/shard_map/cnh,hg->cng/dot_general | solution.py:375
  102.6 0.3 multiply_reduce_fusion.2
  103.0 0.4 copy-done.6
  103.3 3.5 %fusion.103 = bf16[1,496,640]{2,1,0:T(8,128)(2,1)S(1)} fusion(f32[640]{0:T(1024)S(1)} %get-tuple-element.16, f32[496]{0:T(512)S(1)} %add_rsqrt_fusion.3, f32[496,640]{1,0:T(8,128)S(1)} %get-tuple-element.22, f32[496]{0:T(512)S(1)} %broadcast_multiply_fusion.3), kind=kLoop, calls=%fused_computation.177 | loop fusion | flops 21585920 | bytes 1911168 | tf_op jit(solution)/shard_map/convert_element_type | solution.py:380
  106.8 1.3 convert_reduce_fusion
  108.1 0.5 fusion.6
  108.6 6.6 %fusion.48 = bf16[1,496,1280]{2,1,0:T(8,128)(2,1)S(1)} fusion(bf16[496,1280]{1,0:T(8,128)(2,1)S(1)} %get-tuple-element.24, f32[1280]{0:T(1024)S(1)} %get-tuple-element.17, f32[496]{0:T(512)S(1)} %add_rsqrt_fusion.2, f32[496]{0:T(512)S(1)} %broadcast_multiply_fusion), kind=kLoop, calls=%fused_computation.72 | loop fusion | flops 43806720 | bytes 2548608 | tf_op jit(solution)/shard_map/convert_element_type | solution.py:361
  115.2 1.3 fusion.111
  116.5 0.3 multiply_reduce_fusion.1
  116.8 4.1 %fusion.44.x_ref = bf16[496,640]{1,0:T(8,128)(2,1)} fusion(f32[496,640]{1,0:T(8,128)S(1)} %get-tuple-element.26, f32[640]{0:T(1024)S(1)} %get-tuple-element.13, f32[496]{0:T(512)S(1)} %add_rsqrt_fusion.1, f32[496]{0:T(512)S(1)} %broadcast_multiply_fusion.2, f32[496]{0:T(512)S(1)} %fusion.108), kind=kLoop, calls=%fused_computation.68 | loop fusion | flops 21903360 | bytes 1913152 | tf_op jit(solution)/shard_map/convert_element_type | solution.py:369
  120.9 20.6 %shard_map.111 = bf16[1008,640]{1,0:T(8,128)(2,1)} custom-call(bf16[496,640]{1,0:T(8,128)(2,1)} %fusion.44.x_ref), custom_call_target="tpu_custom_call" | custom-call | tf_op jit(solution)/shard_map/pallas_call | solution.py:112
  141.5 2.2 %fusion.82 = f32[496,640]{1,0:T(8,128)S(1)} fusion(bf16[2,5,640,640]{3,2,1,0:T(8,128)(2,1)} %get-tuple-element.11, bf16[1,1008,640]{2,1,0:T(8,128)(2,1)} %bitcast.120), kind=kOutput, calls=%fused_computation.146 | convolution fusion | flops 406323200 | bytes 2723840 | tf_op jit(solution)/shard_map/cnh,hg->cng/dot_general | solution.py:375
  143.7 1.9 %convolution_add_fusion.5 = f32[496,640]{1,0:T(8,128)S(1)} fusion(f32[496,640]{1,0:T(8,128)S(1)} %fusion.82, bf16[2,5,640,640]{3,2,1,0:T(8,128)(2,1)} %get-tuple-element.11, bf16[1,1008,640]{2,1,0:T(8,128)(2,1)S(1)} %bitcast.121), kind=kOutput, calls=%fused_computation.53 | convolution fusion | flops 406640640 | bytes 3993600 | tf_op jit(solution)/shard_map/cnh,hg->cng/dot_general | solution.py:375
  145.7 1.9 %convolution_add_fusion.4 = f32[496,640]{1,0:T(8,128)S(1)} fusion(f32[496,640]{1,0:T(8,128)S(1)} %convolution_add_fusion.5, bf16[2,5,640,640]{3,2,1,0:T(8,128)(2,1)} %get-tuple-element.11, bf16[1,1008,640]{2,1,0:T(8,128)(2,1)S(1)} %bitcast.122), kind=kOutput, calls=%fused_computation.52 | convolution fusion | flops 406640640 | bytes 3993600 | tf_op jit(solution)/shard_map/cnh,hg->cng/dot_general | solution.py:375
  147.6 1.9 %convolution_add_fusion.3 = f32[496,640]{1,0:T(8,128)S(1)} fusion(f32[496,640]{1,0:T(8,128)S(1)} %convolution_add_fusion.4, bf16[2,5,640,640]{3,2,1,0:T(8,128)(2,1)} %get-tuple-element.11, bf16[1,1008,640]{2,1,0:T(8,128)(2,1)S(1)} %bitcast.123), kind=kOutput, calls=%fused_computation.51 | convolution fusion | flops 406640640 | bytes 3993600 | tf_op jit(solution)/shard_map/cnh,hg->cng/dot_general | solution.py:375
  149.5 2.2 %fusion.112 = (f32[496]{0:T(512)S(1)}, f32[496,640]{1,0:T(8,128)S(1)}) fusion(f32[496,640]{1,0:T(8,128)S(1)} %convolution_add_fusion.3, bf16[2,5,640,640]{3,2,1,0:T(8,128)(2,1)} %get-tuple-element.11, bf16[1,1008,640]{2,1,0:T(8,128)(2,1)S(1)} %bitcast.124), kind=kOutput, calls=%fused_computation.203 | convolution fusion | flops 406957568 | bytes 3995584 | tf_op jit(solution)/shard_map/cnh,hg->cng/dot_general | solution.py:375
  151.7 0.3 multiply_reduce_fusion
  152.0 3.5 %fusion.102 = bf16[1,496,640]{2,1,0:T(8,128)(2,1)S(1)} fusion(f32[640]{0:T(1024)S(1)} %get-tuple-element.15, f32[496]{0:T(512)S(1)} %add_rsqrt_fusion, f32[496,640]{1,0:T(8,128)S(1)} %get-tuple-element.28, f32[496]{0:T(512)S(1)} %broadcast_multiply_fusion.1), kind=kLoop, calls=%fused_computation.176 | loop fusion | flops 21585920 | bytes 1911168 | tf_op jit(solution)/shard_map/convert_element_type | solution.py:380
  155.5 2.2 %fusion.5 = bf16[1,496,1280]{2,1,0:T(8,128)(2,1)} fusion(bf16[496,1280]{1,0:T(8,128)(2,1)S(1)} %get-tuple-element.24, bf16[2,640,1280]{2,1,0:T(8,128)(2,1)S(1)} %copy-done.8, bf16[1,496,640]{2,1,0:T(8,128)(2,1)S(1)} %fusion.102), kind=kOutput, calls=%fused_computation.11 | convolution fusion | flops 814551040 | bytes 4812800 | tf_op jit(solution)/shard_map/cnh,hd->cnd/dot_general | solution.py:383
  (31 shorter events, 0.4 us)
Async XLA Ops:
  0.0 0.9 copy-start
  0.0 3.9 %copy-start.4 = (f32[2,1280]{1,0:T(2,128)S(1)}, f32[2,1280]{1,0:T(2,128)}, u32[]{:S(2)}) copy-start(f32[2,1280]{1,0:T(2,128)} %param.16) | copy-start | bytes 30724
  72.7 0.7 copy-start.5
  92.5 2.2 %copy-start.1 = (bf16[752,640]{1,0:T(8,128)(2,1)S(1)}, bf16[752,640]{1,0:T(8,128)(2,1)}, u32[]{:S(2)}) copy-start(bf16[752,640]{1,0:T(8,128)(2,1)} %shard_map.110) | copy-start | bytes 2887684
  100.4 6.4 %copy-start.7 = (bf16[2,640,1280]{2,1,0:T(8,128)(2,1)S(1)}, bf16[2,640,1280]{2,1,0:T(8,128)(2,1)}, u32[]{:S(2)}) copy-start(bf16[2,640,1280]{2,1,0:T(8,128)(2,1)} %get-tuple-element.12) | copy-start | bytes 9830404
  102.6 0.7 copy-start.6
  102.9 3.9 %copy-start.3 = (bf16[496,1280]{1,0:T(8,128)(2,1)S(1)}, bf16[496,1280]{1,0:T(8,128)(2,1)}, u32[]{:S(2)}) copy-start(bf16[496,1280]{1,0:T(8,128)(2,1)} %fusion.2.hidden_ref) | copy-start | bytes 3809284
  108.1 7.1 %copy-start.9 = (bf16[2,1280,640]{2,1,0:T(8,128)(2,1)S(1)}, bf16[2,1280,640]{2,1,0:T(8,128)(2,1)}, u32[]{:S(2)}) copy-start(bf16[2,1280,640]{2,1,0:T(8,128)(2,1)} %get-tuple-element.10) | copy-start | bytes 9830404
  141.5 2.2 %copy-start.2 = (bf16[1008,640]{1,0:T(8,128)(2,1)S(1)}, bf16[1008,640]{1,0:T(8,128)(2,1)}, u32[]{:S(2)}) copy-start(bf16[1008,640]{1,0:T(8,128)(2,1)} %shard_map.111) | copy-start | bytes 3870724
  149.5 6.0 %copy-start.8 = (bf16[2,640,1280]{2,1,0:T(8,128)(2,1)S(1)}, bf16[2,640,1280]{2,1,0:T(8,128)(2,1)}, u32[]{:S(2)}) copy-start(bf16[2,640,1280]{2,1,0:T(8,128)(2,1)} %get-tuple-element.12) | copy-start | bytes 9830404
